TPU v7x, 32 devices: a whole 2x2x4 slice. The times are simulated.
32 devices in a mesh: dp: 4 (over y, x), ctx: 8 (over z, core).
Axes of the slice: x: 2, y: 2, z: 4, core: 2. Of those that a mesh axis runs over, the one named last changes fastest.
Arguments:
- block_input: float32 [4, 1024, 768], P('dp', 'ctx'), may hold values from -6 to 6
- out_cotangent: float32 [4, 1024, 768], P('dp', 'ctx'), may hold values from -6 to 6
- first_gain: float32 [768], replicated, may hold values from 0.25 to 1.75
- first_shift: float32 [768], replicated, may hold values from -3 to 3
- mix_weight: bfloat16 [768, 2304], P('dp'), may hold values from -0.21875 to 0.21875
- query_bias: float32 [768], replicated, may hold values from -3 to 3
- value_bias: float32 [768], replicated, may hold values from -3 to 3
- attn_weight: bfloat16 [768, 768], P('dp'), may hold values from -0.75 to 0.75
- attn_bias: float32 [768], replicated, may hold values from -3 to 3
- second_gain: float32 [768], replicated, may hold values from 0.25 to 1.75
- second_shift: float32 [768], replicated, may hold values from -3 to 3
- up_weight: bfloat16 [768, 3072], P('dp'), may hold values from -0.21875 to 0.21875
- up_bias: float32 [3072], replicated, may hold values from -3 to 3
- down_weight: bfloat16 [3072, 768], P('dp'), may hold values from -0.109375 to 0.109375
- down_bias: float32 [768], replicated, may hold values from -3 to 3
Outputs:
- block_output: float32 [4, 1024, 768], P('dp', 'ctx')
- input_grad: float32 [4, 1024, 768], P('dp', 'ctx')
- first_gain_grad: float32 [768], replicated
- first_shift_grad: float32 [768], replicated
- mix_weight_grad: float32 [768, 2304], P('dp')
- query_bias_grad: float32 [768], replicated
- value_bias_grad: float32 [768], replicated
- attn_weight_grad: float32 [768, 768], P('dp')
- attn_bias_grad: float32 [768], replicated
- second_gain_grad: float32 [768], replicated
- second_shift_grad: float32 [768], replicated
- up_weight_grad: float32 [768, 3072], P('dp')
- up_bias_grad: float32 [3072], replicated
- down_weight_grad: float32 [3072, 768], P('dp')
- down_bias_grad: float32 [768], replicated
All inputs are finite; a program needn't handle non-finite values.
Results may differ from a plain program's by a relative error of at most 0.023.
Values may be sent and summed in bfloat16 or wider, within the bound.
A program may use at most 128 MiB of HBM per device.

v0:
```python
import math
import jax
import jax.numpy as jnp
from jax import lax
from jax.sharding import PartitionSpec as P

H = 12
HD = 64
EPS = 1e-05
GELU_C = math.sqrt(2.0 / math.pi)


def from_behind(value, axis, steps):
    count = lax.axis_size(axis)
    pairs = [(source, (source + steps) % count) for source in range(count)]
    return lax.ppermute(value, axis, pairs)


def layer_norm(x, gain, shift):
    centered = x - jnp.mean(x, axis=-1, keepdims=True)
    rstd = lax.rsqrt(jnp.mean(centered * centered, axis=-1, keepdims=True) + EPS)
    x_hat = centered * rstd
    return (x_hat, rstd, x_hat * gain + shift)


def norm_back(grad, x_hat, rstd, gain):
    g = grad * gain
    return rstd * (
        g
        - jnp.mean(g, axis=-1, keepdims=True)
        - x_hat * jnp.mean(g * x_hat, axis=-1, keepdims=True)
    )


def gelu_pair(u):
    inner = GELU_C * (u + 0.044715 * u * u * u)
    t = jnp.tanh(inner)
    value = 0.5 * u * (1.0 + t)
    slope = 0.5 * (1.0 + t) + 0.5 * u * (1.0 - t * t) * GELU_C * (1.0 + 3.0 * 0.044715 * u * u)
    return (value, slope)


def matmul(a, b):
    return jnp.dot(a, b, preferred_element_type=jnp.float32)


def matmul_tn(a, b):
    return lax.dot_general(a, b, (((0,), (0,)), ((), ())), preferred_element_type=jnp.float32)


def matmul_nt(a, b):
    return lax.dot_general(a, b, (((1,), (1,)), ((), ())), preferred_element_type=jnp.float32)


def body(
    block_input,
    out_cotangent,
    first_gain,
    first_shift,
    mix_weight,
    query_bias,
    value_bias,
    attn_weight,
    attn_bias,
    second_gain,
    second_shift,
    up_weight,
    up_bias,
    down_weight,
    down_bias,
):
    rows = block_input.shape[1]
    width = block_input.shape[2]
    scale = HD ** (-0.5)
    x_rows = block_input.reshape(rows, width)
    cot = out_cotangent.reshape(rows, width)
    mix_full, attn_full, up_full, down_full = (
        lax.all_gather(mix_weight, "dp", axis=0, tiled=True),
        lax.all_gather(attn_weight, "dp", axis=0, tiled=True),
        lax.all_gather(up_weight, "dp", axis=0, tiled=True),
        lax.all_gather(down_weight, "dp", axis=0, tiled=True),
    )
    first_hat, first_rstd, first_out = layer_norm(x_rows, first_gain, first_shift)
    first_in = first_out.astype(jnp.bfloat16)
    mixed = matmul(first_in, mix_full)
    queries = (mixed[:, :width] + query_bias).astype(jnp.bfloat16)
    keys = mixed[:, width : 2 * width].astype(jnp.bfloat16)
    values = (mixed[:, 2 * width :] + value_bias).astype(jnp.bfloat16)
    q3 = queries.reshape(rows, H, HD)
    me = lax.axis_index("ctx")
    cycle_size = lax.axis_size("ctx")
    q_pos = me * rows + jnp.arange(rows)
    q_last = me * rows + rows - 1
    start_state = (
        jnp.full((H, rows), -1e30, jnp.float32),
        jnp.zeros((H, rows), jnp.float32),
        jnp.zeros((H, rows, HD), jnp.float32),
    )
    carry = start_state
    key_piece = lax.all_gather(keys, "ctx", axis=0, tiled=True)
    value_piece = lax.all_gather(values, "ctx", axis=0, tiled=True)
    count = key_piece.shape[0]
    kblock = math.gcd(count, 512)
    nblocks = count // kblock
    key_blocks = key_piece.reshape(nblocks, kblock, H, HD)
    value_blocks = value_piece.reshape(nblocks, kblock, H, HD)
    offsets = jnp.arange(nblocks) * kblock

    def one_block(state, item):
        key_blk, value_blk, offset = item

        def compute(state_in):
            run_max, run_total, run_acc = state_in
            key_pos = offset + jnp.arange(kblock)
            allowed = (key_pos[None, :] <= q_pos[:, None])[None]
            scores = (
                jnp.einsum("qhd,khd->hqk", q3, key_blk, preferred_element_type=jnp.float32) * scale
            )
            scores = jnp.where(allowed, scores, -1e30)
            new_max = jnp.maximum(run_max, jnp.max(scores, axis=-1))
            expo = jnp.where(allowed, jnp.exp(scores - new_max[..., None]), 0.0)
            factor = jnp.exp(run_max - new_max)
            new_total = run_total * factor + jnp.sum(expo, axis=-1)
            new_acc = run_acc * factor[..., None] + jnp.einsum(
                "hqk,khd->hqd", expo, value_blk.astype(jnp.float32), precision=lax.Precision.HIGHEST
            )
            return (new_max, new_total, new_acc)

        def keep_state(state_in):
            return state_in

        return (lax.cond(offset <= q_last, compute, keep_state, state), None)

    carry, unused = lax.scan(one_block, carry, (key_blocks, value_blocks, offsets))
    run_max, run_total, run_acc = carry
    attended = (
        (run_acc / run_total[..., None])
        .transpose(1, 0, 2)
        .reshape(rows, width)
        .astype(jnp.bfloat16)
    )
    lse = run_max + jnp.log(run_total)
    after_attn = x_rows + matmul(attended, attn_full) + attn_bias
    second_hat, second_rstd, second_out = layer_norm(after_attn, second_gain, second_shift)
    second_in = second_out.astype(jnp.bfloat16)
    pre_act = matmul(second_in, up_full) + up_bias
    act_value, act_slope = gelu_pair(pre_act)
    activ = act_value.astype(jnp.bfloat16)
    block_output = after_attn + matmul(activ, down_full) + down_bias
    mix_back, attn_back, up_back, down_back = (
        lax.all_gather(mix_weight, "dp", axis=0, tiled=True),
        lax.all_gather(attn_weight, "dp", axis=0, tiled=True),
        lax.all_gather(up_weight, "dp", axis=0, tiled=True),
        lax.all_gather(down_weight, "dp", axis=0, tiled=True),
    )
    cot_b = cot.astype(jnp.bfloat16)
    down_weight_grad = matmul_tn(activ, cot_b)
    down_bias_grad = jnp.sum(cot, axis=0)
    pre_grad = matmul_nt(cot_b, down_back) * act_slope
    pre_grad_b = pre_grad.astype(jnp.bfloat16)
    up_weight_grad = matmul_tn(second_in, pre_grad_b)
    up_bias_grad = jnp.sum(pre_grad, axis=0)
    second_grad = matmul_nt(pre_grad_b, up_back)
    second_gain_grad = jnp.sum(second_grad * second_hat, axis=0)
    second_shift_grad = jnp.sum(second_grad, axis=0)
    resid_grad = cot + norm_back(second_grad, second_hat, second_rstd, second_gain)
    resid_b = resid_grad.astype(jnp.bfloat16)
    attn_weight_grad = matmul_tn(attended, resid_b)
    attn_bias_grad = jnp.sum(resid_grad, axis=0)
    attended_grad = matmul_nt(resid_b, attn_back).astype(jnp.bfloat16)
    grad3 = attended_grad.reshape(rows, H, HD)
    delta = jnp.sum(
        grad3.astype(jnp.float32) * attended.astype(jnp.float32).reshape(rows, H, HD), axis=-1
    ).T

    def block_grads(key_blk, value_blk, key_start):
        count = key_blk.shape[0]
        key3 = key_blk.reshape(count, H, HD)
        value3 = value_blk.reshape(count, H, HD)
        key_pos = key_start + jnp.arange(count)
        allowed = (key_pos[None, :] <= q_pos[:, None])[None]
        scores = jnp.einsum("qhd,khd->hqk", q3, key3, preferred_element_type=jnp.float32) * scale
        probs = jnp.where(allowed, jnp.exp(scores - lse[..., None]), 0.0)
        dprob = jnp.einsum("qhd,khd->hqk", grad3, value3, preferred_element_type=jnp.float32)
        dscore = probs * (dprob - delta[..., None])
        probs_b = probs.astype(jnp.bfloat16)
        dscore_b = dscore.astype(jnp.bfloat16)
        value_add = jnp.einsum("hqk,qhd->khd", probs_b, grad3, preferred_element_type=jnp.float32)
        key_add = (
            jnp.einsum("hqk,qhd->khd", dscore_b, q3, preferred_element_type=jnp.float32) * scale
        )
        query_add = (
            jnp.einsum("hqk,khd->qhd", dscore_b, key3, preferred_element_type=jnp.float32) * scale
        )
        return (
            query_add.reshape(rows, width),
            key_add.reshape(count, width),
            value_add.reshape(count, width),
        )

    def skip_grads(key_blk, value_blk, key_start):
        count = key_blk.shape[0]
        empty = jnp.zeros((count, width), jnp.float32)
        return (jnp.zeros((rows, width), jnp.float32), empty, empty)

    zeros = jnp.zeros((rows, width), jnp.float32)

    def pass_grads(key_acc, value_acc):
        return (
            from_behind(key_acc.astype(jnp.bfloat16), "ctx", -1).astype(key_acc.dtype),
            from_behind(value_acc.astype(jnp.bfloat16), "ctx", -1).astype(value_acc.dtype),
        )

    def cycle_turn(step, state):
        key_blk, value_blk, key_acc, value_acc, query_acc = state
        owner = (me + step) % cycle_size
        query_add, key_add, value_add = lax.cond(
            owner <= me, block_grads, skip_grads, key_blk, value_blk, owner * rows
        )
        key_blk, value_blk = from_behind((key_blk, value_blk), "ctx", -1)
        key_acc, value_acc = pass_grads(key_acc + key_add, value_acc + value_add)
        return (key_blk, value_blk, key_acc, value_acc, query_acc + query_add)

    key_blk, value_blk, key_acc, value_acc, query_acc = lax.fori_loop(
        0, cycle_size - 1, cycle_turn, (keys, values, zeros, zeros, zeros)
    )
    last_owner = (me + cycle_size - 1) % cycle_size
    query_add, key_add, value_add = lax.cond(
        last_owner <= me, block_grads, skip_grads, key_blk, value_blk, last_owner * rows
    )
    key_grad, value_grad = pass_grads(key_acc + key_add, value_acc + value_add)
    query_grad = query_acc + query_add
    query_bias_grad = jnp.sum(query_grad, axis=0)
    value_bias_grad = jnp.sum(value_grad, axis=0)
    mixed_grad = jnp.concatenate([query_grad, key_grad, value_grad], axis=1).astype(jnp.bfloat16)
    mix_weight_grad = matmul_tn(first_in, mixed_grad)
    first_grad = matmul_nt(mixed_grad, mix_back)
    first_gain_grad = jnp.sum(first_grad * first_hat, axis=0)
    first_shift_grad = jnp.sum(first_grad, axis=0)
    input_grad = resid_grad + norm_back(first_grad, first_hat, first_rstd, first_gain)
    local_mats = (mix_weight_grad, attn_weight_grad, up_weight_grad, down_weight_grad)
    shard_sums = (
        lax.psum_scatter(
            local_mats[0].astype(jnp.bfloat16), "dp", scatter_dimension=0, tiled=True
        ).astype(jnp.float32),
        lax.psum_scatter(
            local_mats[1].astype(jnp.bfloat16), "dp", scatter_dimension=0, tiled=True
        ).astype(jnp.float32),
        lax.psum_scatter(
            local_mats[2].astype(jnp.bfloat16), "dp", scatter_dimension=0, tiled=True
        ).astype(jnp.float32),
        lax.psum_scatter(
            local_mats[3].astype(jnp.bfloat16), "dp", scatter_dimension=0, tiled=True
        ).astype(jnp.float32),
    )
    mats = (
        lax.psum(shard_sums[0].astype(jnp.bfloat16), "ctx").astype(jnp.float32),
        lax.psum(shard_sums[1].astype(jnp.bfloat16), "ctx").astype(jnp.float32),
        lax.psum(shard_sums[2].astype(jnp.bfloat16), "ctx").astype(jnp.float32),
        lax.psum(shard_sums[3].astype(jnp.bfloat16), "ctx").astype(jnp.float32),
    )
    smalls = lax.psum(
        (
            first_gain_grad,
            first_shift_grad,
            query_bias_grad,
            value_bias_grad,
            attn_bias_grad,
            second_gain_grad,
            second_shift_grad,
            up_bias_grad,
            down_bias_grad,
        ),
        ("dp", "ctx"),
    )
    return (
        block_output.reshape(1, rows, width),
        input_grad.reshape(1, rows, width),
        smalls[0],
        smalls[1],
        mats[0],
        smalls[2],
        smalls[3],
        mats[1],
        smalls[4],
        smalls[5],
        smalls[6],
        mats[2],
        smalls[7],
        mats[3],
        smalls[8],
    )


def solution(mesh):
    placed = (
        P("dp", "ctx", None),
        P("dp", "ctx", None),
        P(),
        P(),
        P("dp", None),
        P(),
        P(),
        P("dp", None),
        P(),
        P(),
        P(),
        P("dp", None),
        P(),
        P("dp", None),
        P(),
    )
    return jax.shard_map(
        body,
        mesh=mesh,
        in_specs=placed,
        out_specs=(
            P("dp", "ctx", None),
            P("dp", "ctx", None),
            P(),
            P(),
            P("dp", None),
            P(),
            P(),
            P("dp", None),
            P(),
            P(),
            P(),
            P("dp", None),
            P(),
            P("dp", None),
            P(),
        ),
        check_vma=False,
    )
```

profile of v0, /device:TPU:0, one launch (start us, length us, event | category | flops | bytes accessed | tf_op | source)
XLA Modules:
  0.0 692.6 jit_solution(13095653264918594262)
XLA Ops:
  10.4 49.4 %all-gather.7.cloned.1.call-done = bf16[768,2304]{1,0:T(8,128)(2,1)} async-done(((bf16[192,2304]{1,0:T(8,128)(2,1)}), bf16[768,2304]{1,0:T(8,128)(2,1)}) %all-gather.7.cloned.1.call-update) | async-done | bytes 3538960 | tf_op jit(solution)/shard_map/all_gather | solution.py:78
  67.7 20.9 %all-gather.9.cloned.1.call-done = bf16[1024,768]{1,0:T(8,128)(2,1)} async-done(((bf16[128,768]{1,0:T(8,128)(2,1)}), bf16[1024,768]{1,0:T(8,128)(2,1)}) %all-gather.9.cloned.1.call-update) | async-done | bytes 1572880 | tf_op jit(solution)/shard_map/all_gather | solution.py:100
  94.4 20.8 %all-gather.11.cloned.1.call-done = bf16[1024,768]{1,0:T(8,128)(2,1)} async-done(((bf16[128,768]{1,0:T(8,128)(2,1)}), bf16[1024,768]{1,0:T(8,128)(2,1)}) %all-gather.11.cloned.1.call-update) | async-done | bytes 1572880 | tf_op jit(solution)/shard_map/all_gather | solution.py:101
  117.8 3.8 reshape.243
  125.4 8.6 %while.39 = (s32[]{:T(128)}, f32[12,128]{1,0:T(8,128)S(1)}, f32[12,128]{1,0:T(8,128)S(1)}, f32[12,128,64]{1,2,0:T(8,128)}, s32[2]{0:T(128)S(1)}, /*index=5*/s32[...) while((s32[]{:T(128)}, f32[12,128]{1,0:T(8,128)S(1)}, ...), condition=%wide.region_7.8_spmd.clone, body=%wide.region_2.7_spmd.clone.sunk | while | flops 714346112 | bytes 21801340 | solution.py:134
  126.6 6.1 conditional.8
  135.1 8.6 %all-gather.13.cloned.1.call-done = bf16[768,768]{1,0:T(8,128)(2,1)} async-done(((bf16[192,768]{1,0:T(8,128)(2,1)}), bf16[768,768]{1,0:T(8,128)(2,1)}) %all-gather.13.cloned.1.call-update) | async-done | bytes 1179664 | tf_op jit(solution)/shard_map/all_gather | solution.py:79
  146.2 56.1 %all-gather.15.cloned.1.call-done = bf16[768,3072]{1,0:T(8,128)(2,1)} async-done(((bf16[192,3072]{1,0:T(8,128)(2,1)}), bf16[768,3072]{1,0:T(8,128)(2,1)}) %all-gather.15.cloned.1.call-update) | async-done | bytes 4718608 | tf_op jit(solution)/shard_map/all_gather | solution.py:80
  202.4 4.3 convolution_add_fusion
  206.7 54.3 %all-gather.17.cloned.1.call-done = bf16[3072,768]{1,0:T(8,128)(2,1)} async-done(((bf16[768,768]{1,0:T(8,128)(2,1)}), bf16[3072,768]{1,0:T(8,128)(2,1)}) %all-gather.17.cloned.1.call-update) | async-done | bytes 4718608 | tf_op jit(solution)/shard_map/all_gather | solution.py:81
  261.0 5.4 fusion.63
  273.4 132.6 %while.40 = (s32[]{:T(128)}, bf16[128,768]{0,1:T(8,128)(2,1)}, bf16[128,768]{0,1:T(8,128)(2,1)}, f32[128,768]{0,1:T(8,128)S(1)}, f32[128,768]{0,1:T(8,128)S(1)},...) while((s32[]{:T(128)}, bf16[128,768]{0,1:T(8,128)(2,1)}, ...), condition=%wide.region_16.17_spmd.clone, body=%wide.region_13.16_spmd.clone.sunk | while | flops 128401680 | bytes 14401084 | solution.py:224
  280.6 5.2 conditional.9
  300.4 5.1 collective-permute-start.2
  312.7 3.7 collective-permute-start
  319.4 5.1 collective-permute-start.2
  331.7 3.7 collective-permute-start
  338.4 5.1 collective-permute-start.2
  350.7 3.7 collective-permute-start
  357.3 5.1 collective-permute-start.2
  369.6 3.7 collective-permute-start
  376.3 5.1 collective-permute-start.2
  388.6 3.7 collective-permute-start
  395.3 5.1 collective-permute-start.2
  406.6 8.9 %collective-permute-start.5 = (bf16[128,768]{0,1:T(8,128)(2,1)S(1)}, bf16[128,768]{0,1:T(8,128)(2,1)S(1)}, u32[]{:S(2)}, u32[]{:S(2)}) collective-permute-start(bf16[128,768]{0,1:T(8,128)(2,1)S(1)} %add_convert_fusion), channel_id=1, source_target_pairs={{0,7},{1,0},{2,1},{3,2},{4,3},{5,4},{6,5},{7,6},{8,15},{9,8},{10,9... | collective-permute-start | bytes 589832 | tf_op jit(solution)/shard_map/ppermute | solution.py:16
  429.7 5.4 convolution_convert_fusion
  435.1 36.4 %reduce-scatter.5.cloned.1.call-done = bf16[192,2304]{1,0:T(8,128)(2,1)} async-done(((bf16[768,2304]{1,0:T(8,128)(2,1)}), bf16[192,2304]{1,0:T(8,128)(2,1)}) %reduce-scatter.5.cloned.1.call-update) | async-done | bytes 884752 | tf_op jit(solution)/shard_map/reduce_scatter | solution.py:243
  471.6 60.0 %reduce-scatter.9.cloned.1.call-done = bf16[192,3072]{1,0:T(8,128)(2,1)} async-done(((bf16[768,3072]{1,0:T(8,128)(2,1)}), bf16[192,3072]{1,0:T(8,128)(2,1)}) %reduce-scatter.9.cloned.1.call-update) | async-done | bytes 1179664 | tf_op jit(solution)/shard_map/reduce_scatter | solution.py:249
  531.6 59.8 %reduce-scatter.11.cloned.1.call-done = bf16[768,768]{1,0:T(8,128)(2,1)} async-done(((bf16[3072,768]{1,0:T(8,128)(2,1)}), bf16[768,768]{1,0:T(8,128)(2,1)}) %reduce-scatter.11.cloned.1.call-update) | async-done | bytes 1179664 | tf_op jit(solution)/shard_map/reduce_scatter | solution.py:252
  592.1 4.8 fusion.46
  598.6 42.0 %all-reduce = (f32[768]{0:T(1024)}, f32[768]{0:T(1024)}, f32[768]{0:T(1024)}, f32[768]{0:T(1024)}, f32[768]{0:T(1024)}, /*index=5*/f32[768]{0:T(1024)}, f32[768]{0:T(1024)}, f32[3072]{0:T(1024)}, f32[768]{0:T(1024)}) all-reduce(f32[768]{0:T(1024)S(1)} %get-tuple-element.662, ...), channel_id=1, replica_groups=mesh['dp'=4,'ctx'=8] {'dp','ctx'}, use_global_device_ids=true, to_apply=%region_22.23 | all-reduce | flops 9216 | bytes 73728 | tf_op jit(solution)/shard_map/psum | solution.py:262
  641.5 37.8 %all-reduce.4.cloned.1.call-done = (bf16[192,2304]{1,0:T(8,128)(2,1)}, bf16[192,768]{1,0:T(8,128)(2,1)}, bf16[192,3072]{1,0:T(8,128)(2,1)}, bf16[768,768]{1,0:T(8,128)(2,1)}) async-done(((bf16[192,2304]{1,0:T(8,128)(2,1)}, bf16[192,768]{1,0:T(8,128)(2,1)}, bf16[192,3072]{1,0:T(8,128)(2,1)}, bf16[768,768]{1,0:T(8,128)(2,1)}), (bf16[192,2304]{1,0:T(8,128)(2,1)}, bf16[192,768]{1,0:T(8,128)(2,1)}, ...) | async-done | bytes 3538960 | tf_op jit(solution)/shard_map/psum | solution.py:257
  (313 shorter events, 148.9 us)
Async XLA Ops:
  7.2 52.5 %all-gather.7.cloned.1.call-start = ((), (), s32[]{:S(2)}) async-start(), calls=%async_computation.4 | async-start | bytes 4423680 | tf_op jit(solution)/shard_map/all_gather | solution.py:78
  7.9 80.7 %all-gather.9.cloned.1.call-start = ((), (), s32[]{:S(2)}) async-start(), calls=%async_computation.5 | async-start | bytes 1769472 | tf_op jit(solution)/shard_map/all_gather | solution.py:100
  63.2 52.1 %all-gather.11.cloned.1.call-start = ((), (), s32[]{:S(2)}) async-start(), calls=%async_computation.6 | async-start | bytes 1769472 | tf_op jit(solution)/shard_map/all_gather | solution.py:101
  64.0 79.7 %all-gather.13.cloned.1.call-start = ((), (), s32[]{:S(2)}) async-start(), calls=%async_computation.7 | async-start | bytes 1474560 | tf_op jit(solution)/shard_map/all_gather | solution.py:79
  64.6 137.7 %all-gather.15.cloned.1.call-start = ((), (), s32[]{:S(2)}) async-start(), calls=%async_computation.8 | async-start | bytes 5898240 | tf_op jit(solution)/shard_map/all_gather | solution.py:80
  65.2 195.8 %all-gather.17.cloned.1.call-start = ((), (), s32[]{:S(2)}) async-start(), calls=%async_computation.9 | async-start | bytes 5898240 | tf_op jit(solution)/shard_map/all_gather | solution.py:81
  65.8 369.4 %reduce-scatter.7.cloned.1.call-start = ((), (), s32[]{:S(2)}) async-start(), calls=%async_computation.11 | async-start | bytes 1474560 | tf_op jit(solution)/shard_map/reduce_scatter | solution.py:246
  273.1 198.4 %reduce-scatter.5.cloned.1.call-start = ((), (), s32[]{:S(2)}) async-start(), calls=%async_computation.10 | async-start | bytes 4423680 | tf_op jit(solution)/shard_map/reduce_scatter | solution.py:243
  275.0 17.1 %collective-permute-start = (bf16[128,768]{0,1:T(8,128)(2,1)}, bf16[128,768]{0,1:T(8,128)(2,1)}, u32[]{:S(2)}, u32[]{:S(2)}) collective-permute-start(bf16[128,768]{0,1:T(8,128)(2,1)} %copy.82), channel_id=1, source_target_pairs={{0,7},{1,0},{2,1},{3,2},{4,3},{5,4},{6,5},{7,6},{8,15},{9,8},{10,9... | collective-permute-start | bytes 589832 | tf_op jit(solution)/shard_map/while/body/eval_jaxpr/ppermute | solution.py:16
  279.2 12.9 %collective-permute-start.1 = (bf16[128,768]{0,1:T(8,128)(2,1)}, bf16[128,768]{0,1:T(8,128)(2,1)}, u32[]{:S(2)}, u32[]{:S(2)}) collective-permute-start(bf16[128,768]{0,1:T(8,128)(2,1)} %copy.83), channel_id=1, source_target_pairs={{0,7},{1,0},{2,1},{3,2},{4,3},{5,4},{6,5},{7,6},{8,15},{9,8},{10,9... | collective-permute-start | bytes 589832 | tf_op jit(solution)/shard_map/while/body/eval_jaxpr/ppermute | solution.py:16
  293.8 17.3 %collective-permute-start = (bf16[128,768]{0,1:T(8,128)(2,1)}, bf16[128,768]{0,1:T(8,128)(2,1)}, u32[]{:S(2)}, u32[]{:S(2)}) collective-permute-start(bf16[128,768]{0,1:T(8,128)(2,1)} %copy.82), channel_id=1, source_target_pairs={{0,7},{1,0},{2,1},{3,2},{4,3},{5,4},{6,5},{7,6},{8,15},{9,8},{10,9... | collective-permute-start | bytes 589832 | tf_op jit(solution)/shard_map/while/body/eval_jaxpr/ppermute | solution.py:16
  299.1 12.0 %collective-permute-start.1 = (bf16[128,768]{0,1:T(8,128)(2,1)}, bf16[128,768]{0,1:T(8,128)(2,1)}, u32[]{:S(2)}, u32[]{:S(2)}) collective-permute-start(bf16[128,768]{0,1:T(8,128)(2,1)} %copy.83), channel_id=1, source_target_pairs={{0,7},{1,0},{2,1},{3,2},{4,3},{5,4},{6,5},{7,6},{8,15},{9,8},{10,9... | collective-permute-start | bytes 589832 | tf_op jit(solution)/shard_map/while/body/eval_jaxpr/ppermute | solution.py:16
  300.4 8.6 %collective-permute-start.2 = (bf16[128,768]{0,1:T(8,128)(2,1)}, bf16[128,768]{0,1:T(8,128)(2,1)S(1)}, u32[]{:S(2)}, u32[]{:S(2)}) collective-permute-start(bf16[128,768]{0,1:T(8,128)(2,1)} %fusion.105), channel_id=1, source_target_pairs={{0,7},{1,0},{2,1},{3,2},{4,3},{5,4},{6,5},{7,6},{8,15},{9,8},{10,9... | collective-permute-start | bytes 589832 | tf_op jit(solution)/shard_map/while/body/eval_jaxpr/ppermute | solution.py:16
  312.7 17.3 %collective-permute-start = (bf16[128,768]{0,1:T(8,128)(2,1)}, bf16[128,768]{0,1:T(8,128)(2,1)}, u32[]{:S(2)}, u32[]{:S(2)}) collective-permute-start(bf16[128,768]{0,1:T(8,128)(2,1)} %copy.82), channel_id=1, source_target_pairs={{0,7},{1,0},{2,1},{3,2},{4,3},{5,4},{6,5},{7,6},{8,15},{9,8},{10,9... | collective-permute-start | bytes 589832 | tf_op jit(solution)/shard_map/while/body/eval_jaxpr/ppermute | solution.py:16
  318.0 12.0 %collective-permute-start.1 = (bf16[128,768]{0,1:T(8,128)(2,1)}, bf16[128,768]{0,1:T(8,128)(2,1)}, u32[]{:S(2)}, u32[]{:S(2)}) collective-permute-start(bf16[128,768]{0,1:T(8,128)(2,1)} %copy.83), channel_id=1, source_target_pairs={{0,7},{1,0},{2,1},{3,2},{4,3},{5,4},{6,5},{7,6},{8,15},{9,8},{10,9... | collective-permute-start | bytes 589832 | tf_op jit(solution)/shard_map/while/body/eval_jaxpr/ppermute | solution.py:16
  319.4 8.6 %collective-permute-start.2 = (bf16[128,768]{0,1:T(8,128)(2,1)}, bf16[128,768]{0,1:T(8,128)(2,1)S(1)}, u32[]{:S(2)}, u32[]{:S(2)}) collective-permute-start(bf16[128,768]{0,1:T(8,128)(2,1)} %fusion.105), channel_id=1, source_target_pairs={{0,7},{1,0},{2,1},{3,2},{4,3},{5,4},{6,5},{7,6},{8,15},{9,8},{10,9... | collective-permute-start | bytes 589832 | tf_op jit(solution)/shard_map/while/body/eval_jaxpr/ppermute | solution.py:16
  331.7 17.3 %collective-permute-start = (bf16[128,768]{0,1:T(8,128)(2,1)}, bf16[128,768]{0,1:T(8,128)(2,1)}, u32[]{:S(2)}, u32[]{:S(2)}) collective-permute-start(bf16[128,768]{0,1:T(8,128)(2,1)} %copy.82), channel_id=1, source_target_pairs={{0,7},{1,0},{2,1},{3,2},{4,3},{5,4},{6,5},{7,6},{8,15},{9,8},{10,9... | collective-permute-start | bytes 589832 | tf_op jit(solution)/shard_map/while/body/eval_jaxpr/ppermute | solution.py:16
  337.0 12.0 %collective-permute-start.1 = (bf16[128,768]{0,1:T(8,128)(2,1)}, bf16[128,768]{0,1:T(8,128)(2,1)}, u32[]{:S(2)}, u32[]{:S(2)}) collective-permute-start(bf16[128,768]{0,1:T(8,128)(2,1)} %copy.83), channel_id=1, source_target_pairs={{0,7},{1,0},{2,1},{3,2},{4,3},{5,4},{6,5},{7,6},{8,15},{9,8},{10,9... | collective-permute-start | bytes 589832 | tf_op jit(solution)/shard_map/while/body/eval_jaxpr/ppermute | solution.py:16
  338.4 8.6 %collective-permute-start.2 = (bf16[128,768]{0,1:T(8,128)(2,1)}, bf16[128,768]{0,1:T(8,128)(2,1)S(1)}, u32[]{:S(2)}, u32[]{:S(2)}) collective-permute-start(bf16[128,768]{0,1:T(8,128)(2,1)} %fusion.105), channel_id=1, source_target_pairs={{0,7},{1,0},{2,1},{3,2},{4,3},{5,4},{6,5},{7,6},{8,15},{9,8},{10,9... | collective-permute-start | bytes 589832 | tf_op jit(solution)/shard_map/while/body/eval_jaxpr/ppermute | solution.py:16
  350.7 17.3 %collective-permute-start = (bf16[128,768]{0,1:T(8,128)(2,1)}, bf16[128,768]{0,1:T(8,128)(2,1)}, u32[]{:S(2)}, u32[]{:S(2)}) collective-permute-start(bf16[128,768]{0,1:T(8,128)(2,1)} %copy.82), channel_id=1, source_target_pairs={{0,7},{1,0},{2,1},{3,2},{4,3},{5,4},{6,5},{7,6},{8,15},{9,8},{10,9... | collective-permute-start | bytes 589832 | tf_op jit(solution)/shard_map/while/body/eval_jaxpr/ppermute | solution.py:16
  356.0 12.0 %collective-permute-start.1 = (bf16[128,768]{0,1:T(8,128)(2,1)}, bf16[128,768]{0,1:T(8,128)(2,1)}, u32[]{:S(2)}, u32[]{:S(2)}) collective-permute-start(bf16[128,768]{0,1:T(8,128)(2,1)} %copy.83), channel_id=1, source_target_pairs={{0,7},{1,0},{2,1},{3,2},{4,3},{5,4},{6,5},{7,6},{8,15},{9,8},{10,9... | collective-permute-start | bytes 589832 | tf_op jit(solution)/shard_map/while/body/eval_jaxpr/ppermute | solution.py:16
  357.3 8.6 %collective-permute-start.2 = (bf16[128,768]{0,1:T(8,128)(2,1)}, bf16[128,768]{0,1:T(8,128)(2,1)S(1)}, u32[]{:S(2)}, u32[]{:S(2)}) collective-permute-start(bf16[128,768]{0,1:T(8,128)(2,1)} %fusion.105), channel_id=1, source_target_pairs={{0,7},{1,0},{2,1},{3,2},{4,3},{5,4},{6,5},{7,6},{8,15},{9,8},{10,9... | collective-permute-start | bytes 589832 | tf_op jit(solution)/shard_map/while/body/eval_jaxpr/ppermute | solution.py:16
  369.6 17.3 %collective-permute-start = (bf16[128,768]{0,1:T(8,128)(2,1)}, bf16[128,768]{0,1:T(8,128)(2,1)}, u32[]{:S(2)}, u32[]{:S(2)}) collective-permute-start(bf16[128,768]{0,1:T(8,128)(2,1)} %copy.82), channel_id=1, source_target_pairs={{0,7},{1,0},{2,1},{3,2},{4,3},{5,4},{6,5},{7,6},{8,15},{9,8},{10,9... | collective-permute-start | bytes 589832 | tf_op jit(solution)/shard_map/while/body/eval_jaxpr/ppermute | solution.py:16
  374.9 12.0 %collective-permute-start.1 = (bf16[128,768]{0,1:T(8,128)(2,1)}, bf16[128,768]{0,1:T(8,128)(2,1)}, u32[]{:S(2)}, u32[]{:S(2)}) collective-permute-start(bf16[128,768]{0,1:T(8,128)(2,1)} %copy.83), channel_id=1, source_target_pairs={{0,7},{1,0},{2,1},{3,2},{4,3},{5,4},{6,5},{7,6},{8,15},{9,8},{10,9... | collective-permute-start | bytes 589832 | tf_op jit(solution)/shard_map/while/body/eval_jaxpr/ppermute | solution.py:16
  376.3 8.6 %collective-permute-start.2 = (bf16[128,768]{0,1:T(8,128)(2,1)}, bf16[128,768]{0,1:T(8,128)(2,1)S(1)}, u32[]{:S(2)}, u32[]{:S(2)}) collective-permute-start(bf16[128,768]{0,1:T(8,128)(2,1)} %fusion.105), channel_id=1, source_target_pairs={{0,7},{1,0},{2,1},{3,2},{4,3},{5,4},{6,5},{7,6},{8,15},{9,8},{10,9... | collective-permute-start | bytes 589832 | tf_op jit(solution)/shard_map/while/body/eval_jaxpr/ppermute | solution.py:16
  388.6 17.3 %collective-permute-start = (bf16[128,768]{0,1:T(8,128)(2,1)}, bf16[128,768]{0,1:T(8,128)(2,1)}, u32[]{:S(2)}, u32[]{:S(2)}) collective-permute-start(bf16[128,768]{0,1:T(8,128)(2,1)} %copy.82), channel_id=1, source_target_pairs={{0,7},{1,0},{2,1},{3,2},{4,3},{5,4},{6,5},{7,6},{8,15},{9,8},{10,9... | collective-permute-start | bytes 589832 | tf_op jit(solution)/shard_map/while/body/eval_jaxpr/ppermute | solution.py:16
  393.9 12.0 %collective-permute-start.1 = (bf16[128,768]{0,1:T(8,128)(2,1)}, bf16[128,768]{0,1:T(8,128)(2,1)}, u32[]{:S(2)}, u32[]{:S(2)}) collective-permute-start(bf16[128,768]{0,1:T(8,128)(2,1)} %copy.83), channel_id=1, source_target_pairs={{0,7},{1,0},{2,1},{3,2},{4,3},{5,4},{6,5},{7,6},{8,15},{9,8},{10,9... | collective-permute-start | bytes 589832 | tf_op jit(solution)/shard_map/while/body/eval_jaxpr/ppermute | solution.py:16
  395.3 8.6 %collective-permute-start.2 = (bf16[128,768]{0,1:T(8,128)(2,1)}, bf16[128,768]{0,1:T(8,128)(2,1)S(1)}, u32[]{:S(2)}, u32[]{:S(2)}) collective-permute-start(bf16[128,768]{0,1:T(8,128)(2,1)} %fusion.105), channel_id=1, source_target_pairs={{0,7},{1,0},{2,1},{3,2},{4,3},{5,4},{6,5},{7,6},{8,15},{9,8},{10,9... | collective-permute-start | bytes 589832 | tf_op jit(solution)/shard_map/while/body/eval_jaxpr/ppermute | solution.py:16
  406.6 12.1 %collective-permute-start.5 = (bf16[128,768]{0,1:T(8,128)(2,1)S(1)}, bf16[128,768]{0,1:T(8,128)(2,1)S(1)}, u32[]{:S(2)}, u32[]{:S(2)}) collective-permute-start(bf16[128,768]{0,1:T(8,128)(2,1)S(1)} %add_convert_fusion), channel_id=1, source_target_pairs={{0,7},{1,0},{2,1},{3,2},{4,3},{5,4},{6,5},{7,6},{8,15},{9,8},{10,9... | collective-permute-start | bytes 589832 | tf_op jit(solution)/shard_map/ppermute | solution.py:16
  423.9 107.7 %reduce-scatter.9.cloned.1.call-start = ((), (), s32[]{:S(2)}) async-start(), calls=%async_computation.12 | async-start | bytes 5898240 | tf_op jit(solution)/shard_map/reduce_scatter | solution.py:249
  428.7 162.7 %reduce-scatter.11.cloned.1.call-start = ((), (), s32[]{:S(2)}) async-start(), calls=%async_computation.13 | async-start | bytes 5898240 | tf_op jit(solution)/shard_map/reduce_scatter | solution.py:252
  435.1 244.3 %all-reduce.4.cloned.1.call-start = ((), (), s32[]{:S(2)}) async-start(), calls=%async_computation.14 | async-start | bytes 7077888 | tf_op jit(solution)/shard_map/psum | solution.py:257
  (52 other events, 1142.0 us)
Sparse Core Ops, SparseCore 0:
  9.9 49.8 all-gather.6
  63.3 25.2 all-gather.8
  90.8 24.3 all-gather.10
  116.9 26.7 all-gather.12
  145.4 56.9 all-gather.14
  204.0 56.9 all-gather.16
  273.2 28.6 reduce-scatter.6
  424.0 47.5 reduce-scatter.4
  474.6 56.9 reduce-scatter.8
  534.4 56.9 reduce-scatter.10
  594.1 85.2 all-reduce.3
where the time goes:
time: 694 us; the launch traced here: 693 us
  waiting for transfers between devices  448 us (65%)
  starting transfers between devices  66.9 us (10%)
  local copies, waits for them, and re-layouts  51.3 us (7%)
  matrix products  45.4 us (7%)
  blocking collectives  42 us (6%)
  other arithmetic  22.7 us (3%)
  between operations  14.4 us (2%)
    ppermute x30, starting transfers between devices, from_behind(): return lax.ppermute(value, axis, pairs)  66.2 us
    reduce_scatter x1, waiting for transfers between devices, body(): lax.psum_scatter(local_mats[2].astype(jnp.bfloat16), 'dp', scatter_dimens...  60 us
    reduce_scatter x1, waiting for transfers between devices, body(): lax.psum_scatter(local_mats[3].astype(jnp.bfloat16), 'dp', scatter_dimens...  59.8 us
    all_gather x1, waiting for transfers between devices, body(): lax.all_gather(up_weight, 'dp', axis=0, tiled=True)  56.1 us
    all_gather x1, waiting for transfers between devices, body(): lax.all_gather(down_weight, 'dp', axis=0, tiled=True)  54.3 us
    all_gather x1, waiting for transfers between devices, body(): lax.all_gather(mix_weight, 'dp', axis=0, tiled=True)  49.4 us
    psum x1, blocking collectives, body(): lax.psum((first_gain_grad, first_shift_grad, query_bias_grad, value_bias_...  42 us
    ppermute x30, waiting for transfers between devices, from_behind(): return lax.ppermute(value, axis, pairs)  41.2 us
  transfers between devices with their start and end apart: 41, of which 26 were waited for; matrix products, arithmetic and copies ran while one was open for 13% of the time, Pallas kernels for 0%

commit v1 on v0

--- a/solution.py
+++ b/solution.py
@@ -254,7 +254,9 @@
         ).astype(jnp.float32),
     )
     mats = (
-        lax.psum(shard_sums[0].astype(jnp.bfloat16), "ctx").astype(jnp.float32),
+        jnp.sum(lax.all_gather(shard_sums[0].astype(jnp.bfloat16), "ctx"), axis=0).astype(
+            jnp.float32
+        ),
         lax.psum(shard_sums[1].astype(jnp.bfloat16), "ctx").astype(jnp.float32),
         lax.psum(shard_sums[2].astype(jnp.bfloat16), "ctx").astype(jnp.float32),
         lax.psum(shard_sums[3].astype(jnp.bfloat16), "ctx").astype(jnp.float32),

time: 694 us -> 633 us (0.912)
  waiting for transfers between devices: 448 us -> 395 us
  local copies, waits for them, and re-layouts: 51.3 us -> 44.3 us
    all_gather x0 -> x1, waiting for transfers between devices: none -> 65.7 us  [body(): lax.all_gather(shard_sums[0].astype(jnp.bfloat16), 'ctx')]
    reduce_scatter x1, waiting for transfers between devices: 60 us -> 0.02 us  [body(): lax.psum_scatter(local_mats[2].astype(jnp.bfloat16), 'dp', scatter_dimens...]
    reduce_scatter x1, waiting for transfers between devices: 59.8 us -> 0.02 us  [body(): lax.psum_scatter(local_mats[3].astype(jnp.bfloat16), 'dp', scatter_dimens...]
    psum x1, waiting for transfers between devices: 37.8 us -> 23.7 us  [body(): lax.psum(shard_sums[1].astype(jnp.bfloat16), 'ctx').astype(jnp.float32)]
    reduce_scatter x1, waiting for transfers between devices: 36.4 us -> 47 us  [body(): lax.psum_scatter(local_mats[0].astype(jnp.bfloat16), 'dp', scatter_dimens...]
  transfers between devices with their start and end apart: 41 -> 42, of which waited for: 26 -> 25; matrix products, arithmetic and copies ran while one was open for 13% -> 15% of each run, Pallas kernels for 0% -> 0%
where the time goes in v1:
time: 633 us; the launch traced here: 632 us
  waiting for transfers between devices  395 us (62%)
  starting transfers between devices  62.8 us (10%)
  local copies, waits for them, and re-layouts  44.3 us (7%)
  matrix products  43 us (7%)
  blocking collectives  41.9 us (7%)
  other arithmetic  27.5 us (4%)
  between operations  14.9 us (2%)
    all_gather x1, waiting for transfers between devices, body(): lax.all_gather(shard_sums[0].astype(jnp.bfloat16), 'ctx')  65.7 us
    ppermute x30, starting transfers between devices, from_behind(): return lax.ppermute(value, axis, pairs)  62.2 us
    all_gather x1, waiting for transfers between devices, body(): lax.all_gather(up_weight, 'dp', axis=0, tiled=True)  55.9 us
    all_gather x1, waiting for transfers between devices, body(): lax.all_gather(down_weight, 'dp', axis=0, tiled=True)  55.3 us
    all_gather x1, waiting for transfers between devices, body(): lax.all_gather(mix_weight, 'dp', axis=0, tiled=True)  49.4 us
    reduce_scatter x1, waiting for transfers between devices, body(): lax.psum_scatter(local_mats[0].astype(jnp.bfloat16), 'dp', scatter_dimens...  47 us
    psum x1, blocking collectives, body(): lax.psum((first_gain_grad, first_shift_grad, query_bias_grad, value_bias_...  41.9 us
    ppermute x30, waiting for transfers between devices, from_behind(): return lax.ppermute(value, axis, pairs)  41.1 us
  transfers between devices with their start and end apart: 42, of which 25 were waited for; matrix products, arithmetic and copies ran while one was open for 15% of the time, Pallas kernels for 0%

profile of v1, /device:TPU:0, one launch (start us, length us, event | category | flops | bytes accessed | tf_op | source)
XLA Modules:
  0.0 631.7 jit_solution(4169378867823712913)
XLA Ops:
  10.4 49.4 %all-gather.9.cloned.1.call-done = bf16[768,2304]{1,0:T(8,128)(2,1)} async-done(((bf16[192,2304]{1,0:T(8,128)(2,1)}), bf16[768,2304]{1,0:T(8,128)(2,1)}) %all-gather.9.cloned.1.call-update) | async-done | bytes 3538960 | tf_op jit(solution)/shard_map/all_gather | solution.py:78
  66.0 22.6 %all-gather.11.cloned.1.call-done = bf16[1024,768]{1,0:T(8,128)(2,1)} async-done(((bf16[128,768]{1,0:T(8,128)(2,1)}), bf16[1024,768]{1,0:T(8,128)(2,1)}) %all-gather.11.cloned.1.call-update) | async-done | bytes 1572880 | tf_op jit(solution)/shard_map/all_gather | solution.py:100
  94.4 20.3 %all-gather.13.cloned.1.call-done = bf16[1024,768]{1,0:T(8,128)(2,1)} async-done(((bf16[128,768]{1,0:T(8,128)(2,1)}), bf16[1024,768]{1,0:T(8,128)(2,1)}) %all-gather.13.cloned.1.call-update) | async-done | bytes 1572880 | tf_op jit(solution)/shard_map/all_gather | solution.py:101
  117.3 3.8 reshape.243
  124.1 7.8 %while.39 = (s32[]{:T(128)}, f32[12,128]{1,0:T(8,128)S(1)}, f32[12,128]{1,0:T(8,128)S(1)}, f32[12,128,64]{1,2,0:T(8,128)S(1)}, s32[2]{0:T(128)S(1)}, /*index=5*/...) while((s32[]{:T(128)}, f32[12,128]{1,0:T(8,128)S(1)}, ...), condition=%wide.region_7.8_spmd.clone, body=%wide.region_2.7_spmd.clone.sunk | while | flops 714346112 | bytes 18655556 | solution.py:134
  125.3 5.2 conditional.8
  131.9 11.2 %all-gather.15.cloned.1.call-done = bf16[768,768]{1,0:T(8,128)(2,1)} async-done(((bf16[192,768]{1,0:T(8,128)(2,1)}), bf16[768,768]{1,0:T(8,128)(2,1)}) %all-gather.15.cloned.1.call-update) | async-done | bytes 1179664 | tf_op jit(solution)/shard_map/all_gather | solution.py:79
  145.9 55.9 %all-gather.17.cloned.1.call-done = bf16[768,3072]{1,0:T(8,128)(2,1)} async-done(((bf16[192,3072]{1,0:T(8,128)(2,1)}), bf16[768,3072]{1,0:T(8,128)(2,1)}) %all-gather.17.cloned.1.call-update) | async-done | bytes 4718608 | tf_op jit(solution)/shard_map/all_gather | solution.py:80
  205.1 55.3 %all-gather.19.cloned.1.call-done = bf16[3072,768]{1,0:T(8,128)(2,1)} async-done(((bf16[768,768]{1,0:T(8,128)(2,1)}), bf16[3072,768]{1,0:T(8,128)(2,1)}) %all-gather.19.cloned.1.call-update) | async-done | bytes 4718608 | tf_op jit(solution)/shard_map/all_gather | solution.py:81
  260.4 4.9 fusion.63
  270.3 4.9 convolution_convert_fusion.1
  275.3 3.7 convolution_convert_fusion
  284.9 124.9 %while.40 = (s32[]{:T(128)}, bf16[128,768]{0,1:T(8,128)(2,1)}, bf16[128,768]{0,1:T(8,128)(2,1)}, f32[128,768]{0,1:T(8,128)S(1)}, f32[128,768]{0,1:T(8,128)S(1)},...) while((s32[]{:T(128)}, bf16[128,768]{0,1:T(8,128)(2,1)}, ...), condition=%wide.region_16.17_spmd.clone, body=%wide.region_13.16_spmd.clone.sunk | while | flops 128401680 | bytes 14401084 | solution.py:224
  291.6 4.6 conditional.9
  304.1 3.7 collective-permute-start
  310.3 4.4 collective-permute-start.2
  322.0 3.7 collective-permute-start
  328.2 4.5 collective-permute-start.2
  339.9 3.7 collective-permute-start
  346.0 4.6 collective-permute-start.2
  357.8 3.7 collective-permute-start
  363.9 4.5 collective-permute-start.2
  375.6 3.7 collective-permute-start
  381.8 4.5 collective-permute-start.2
  399.7 4.5 collective-permute-start.2
  410.0 8.3 %collective-permute-start.5 = (bf16[128,768]{0,1:T(8,128)(2,1)S(1)}, bf16[128,768]{0,1:T(8,128)(2,1)S(1)}, u32[]{:S(2)}, u32[]{:S(2)}) collective-permute-start(bf16[128,768]{0,1:T(8,128)(2,1)S(1)} %add_convert_fusion), channel_id=1, source_target_pairs={{0,7},{1,0},{2,1},{3,2},{4,3},{5,4},{6,5},{7,6},{8,15},{9,8},{10,9... | collective-permute-start | bytes 589832 | tf_op jit(solution)/shard_map/ppermute | solution.py:16
  427.4 47.0 %reduce-scatter.5.cloned.1.call-done = bf16[192,2304]{1,0:T(8,128)(2,1)} async-done(((bf16[768,2304]{1,0:T(8,128)(2,1)}), bf16[192,2304]{1,0:T(8,128)(2,1)}) %reduce-scatter.5.cloned.1.call-update) | async-done | bytes 884752 | tf_op jit(solution)/shard_map/reduce_scatter | solution.py:243
  474.6 4.3 fusion.46
  480.5 41.9 %all-reduce = (f32[768]{0:T(1024)}, f32[768]{0:T(1024)}, f32[768]{0:T(1024)}, f32[768]{0:T(1024)}, f32[768]{0:T(1024)}, /*index=5*/f32[768]{0:T(1024)}, f32[768]{0:T(1024)}, f32[3072]{0:T(1024)}, f32[768]{0:T(1024)}) all-reduce(f32[768]{0:T(1024)S(1)} %get-tuple-element.662, ...), channel_id=1, replica_groups=mesh['dp'=4,'ctx'=8] {'dp','ctx'}, use_global_device_ids=true, to_apply=%region_22.23 | all-reduce | flops 9216 | bytes 73728 | tf_op jit(solution)/shard_map/psum | solution.py:264
  523.3 23.7 %all-reduce.4.cloned.1.call-done = (bf16[192,768]{1,0:T(8,128)(2,1)}, bf16[192,3072]{1,0:T(8,128)(2,1)}, bf16[768,768]{1,0:T(8,128)(2,1)}) async-done(((bf16[192,768]{1,0:T(8,128)(2,1)}, bf16[192,3072]{1,0:T(8,128)(2,1)}, bf16[768,768]{1,0:T(8,128)(2,1)}), (bf16[192,768]{1,0:T(8,128)(2,1)}, bf16[192,3072]{1,0:T(8,128)(2,1)}, bf16[768,768]{1,0:T(8,128)(2,1)})) %all-reduce.4.cloned.1.call-update) | async-done | bytes 2654224 | tf_op jit(solution)/shard_map/psum | solution.py:260
  553.4 65.7 %all-gather.21.cloned.1.call-done = bf16[1536,2304]{1,0:T(8,128)(2,1)} async-done(((bf16[192,2304]{1,0:T(8,128)(2,1)}), bf16[1536,2304]{1,0:T(8,128)(2,1)}) %all-gather.21.cloned.1.call-update) | async-done | bytes 7077904 | tf_op jit(solution)/shard_map/all_gather | solution.py:257
  619.1 4.4 reduce_sum.196
  (311 shorter events, 142.5 us)
Async XLA Ops:
  7.2 52.5 %all-gather.9.cloned.1.call-start = ((), (), s32[]{:S(2)}) async-start(), calls=%async_computation.4 | async-start | bytes 4423680 | tf_op jit(solution)/shard_map/all_gather | solution.py:78
  7.9 80.7 %all-gather.11.cloned.1.call-start = ((), (), s32[]{:S(2)}) async-start(), calls=%async_computation.5 | async-start | bytes 1769472 | tf_op jit(solution)/shard_map/all_gather | solution.py:100
  63.2 51.5 %all-gather.13.cloned.1.call-start = ((), (), s32[]{:S(2)}) async-start(), calls=%async_computation.6 | async-start | bytes 1769472 | tf_op jit(solution)/shard_map/all_gather | solution.py:101
  64.0 79.1 %all-gather.15.cloned.1.call-start = ((), (), s32[]{:S(2)}) async-start(), calls=%async_computation.7 | async-start | bytes 1474560 | tf_op jit(solution)/shard_map/all_gather | solution.py:79
  64.6 137.2 %all-gather.17.cloned.1.call-start = ((), (), s32[]{:S(2)}) async-start(), calls=%async_computation.8 | async-start | bytes 5898240 | tf_op jit(solution)/shard_map/all_gather | solution.py:80
  65.2 195.3 %all-gather.19.cloned.1.call-start = ((), (), s32[]{:S(2)}) async-start(), calls=%async_computation.9 | async-start | bytes 5898240 | tf_op jit(solution)/shard_map/all_gather | solution.py:81
  65.8 360.9 %reduce-scatter.7.cloned.1.call-start = ((), (), s32[]{:S(2)}) async-start(), calls=%async_computation.11 | async-start | bytes 1474560 | tf_op jit(solution)/shard_map/reduce_scatter | solution.py:246
  270.1 156.7 %reduce-scatter.9.cloned.1.call-start = ((), (), s32[]{:S(2)}) async-start(), calls=%async_computation.12 | async-start | bytes 5898240 | tf_op jit(solution)/shard_map/reduce_scatter | solution.py:249
  275.2 151.5 %reduce-scatter.11.cloned.1.call-start = ((), (), s32[]{:S(2)}) async-start(), calls=%async_computation.13 | async-start | bytes 5898240 | tf_op jit(solution)/shard_map/reduce_scatter | solution.py:252
  279.1 195.4 %reduce-scatter.5.cloned.1.call-start = ((), (), s32[]{:S(2)}) async-start(), calls=%async_computation.10 | async-start | bytes 4423680 | tf_op jit(solution)/shard_map/reduce_scatter | solution.py:243
  286.5 15.9 %collective-permute-start = (bf16[128,768]{0,1:T(8,128)(2,1)}, bf16[128,768]{0,1:T(8,128)(2,1)}, u32[]{:S(2)}, u32[]{:S(2)}) collective-permute-start(bf16[128,768]{0,1:T(8,128)(2,1)} %copy.82), channel_id=1, source_target_pairs={{0,7},{1,0},{2,1},{3,2},{4,3},{5,4},{6,5},{7,6},{8,15},{9,8},{10,9... | collective-permute-start | bytes 589832 | tf_op jit(solution)/shard_map/while/body/eval_jaxpr/ppermute | solution.py:16
  290.7 11.7 %collective-permute-start.1 = (bf16[128,768]{0,1:T(8,128)(2,1)}, bf16[128,768]{0,1:T(8,128)(2,1)}, u32[]{:S(2)}, u32[]{:S(2)}) collective-permute-start(bf16[128,768]{0,1:T(8,128)(2,1)} %copy.83), channel_id=1, source_target_pairs={{0,7},{1,0},{2,1},{3,2},{4,3},{5,4},{6,5},{7,6},{8,15},{9,8},{10,9... | collective-permute-start | bytes 589832 | tf_op jit(solution)/shard_map/while/body/eval_jaxpr/ppermute | solution.py:16
  304.1 16.2 %collective-permute-start = (bf16[128,768]{0,1:T(8,128)(2,1)}, bf16[128,768]{0,1:T(8,128)(2,1)}, u32[]{:S(2)}, u32[]{:S(2)}) collective-permute-start(bf16[128,768]{0,1:T(8,128)(2,1)} %copy.82), channel_id=1, source_target_pairs={{0,7},{1,0},{2,1},{3,2},{4,3},{5,4},{6,5},{7,6},{8,15},{9,8},{10,9... | collective-permute-start | bytes 589832 | tf_op jit(solution)/shard_map/while/body/eval_jaxpr/ppermute | solution.py:16
  309.5 10.8 %collective-permute-start.1 = (bf16[128,768]{0,1:T(8,128)(2,1)}, bf16[128,768]{0,1:T(8,128)(2,1)}, u32[]{:S(2)}, u32[]{:S(2)}) collective-permute-start(bf16[128,768]{0,1:T(8,128)(2,1)} %copy.83), channel_id=1, source_target_pairs={{0,7},{1,0},{2,1},{3,2},{4,3},{5,4},{6,5},{7,6},{8,15},{9,8},{10,9... | collective-permute-start | bytes 589832 | tf_op jit(solution)/shard_map/while/body/eval_jaxpr/ppermute | solution.py:16
  322.0 16.2 %collective-permute-start = (bf16[128,768]{0,1:T(8,128)(2,1)}, bf16[128,768]{0,1:T(8,128)(2,1)}, u32[]{:S(2)}, u32[]{:S(2)}) collective-permute-start(bf16[128,768]{0,1:T(8,128)(2,1)} %copy.82), channel_id=1, source_target_pairs={{0,7},{1,0},{2,1},{3,2},{4,3},{5,4},{6,5},{7,6},{8,15},{9,8},{10,9... | collective-permute-start | bytes 589832 | tf_op jit(solution)/shard_map/while/body/eval_jaxpr/ppermute | solution.py:16
  327.3 10.9 %collective-permute-start.1 = (bf16[128,768]{0,1:T(8,128)(2,1)}, bf16[128,768]{0,1:T(8,128)(2,1)}, u32[]{:S(2)}, u32[]{:S(2)}) collective-permute-start(bf16[128,768]{0,1:T(8,128)(2,1)} %copy.83), channel_id=1, source_target_pairs={{0,7},{1,0},{2,1},{3,2},{4,3},{5,4},{6,5},{7,6},{8,15},{9,8},{10,9... | collective-permute-start | bytes 589832 | tf_op jit(solution)/shard_map/while/body/eval_jaxpr/ppermute | solution.py:16
  328.2 8.0 %collective-permute-start.2 = (bf16[128,768]{0,1:T(8,128)(2,1)}, bf16[128,768]{0,1:T(8,128)(2,1)S(1)}, u32[]{:S(2)}, u32[]{:S(2)}) collective-permute-start(bf16[128,768]{0,1:T(8,128)(2,1)} %fusion.105), channel_id=1, source_target_pairs={{0,7},{1,0},{2,1},{3,2},{4,3},{5,4},{6,5},{7,6},{8,15},{9,8},{10,9... | collective-permute-start | bytes 589832 | tf_op jit(solution)/shard_map/while/body/eval_jaxpr/ppermute | solution.py:16
  339.9 16.3 %collective-permute-start = (bf16[128,768]{0,1:T(8,128)(2,1)}, bf16[128,768]{0,1:T(8,128)(2,1)}, u32[]{:S(2)}, u32[]{:S(2)}) collective-permute-start(bf16[128,768]{0,1:T(8,128)(2,1)} %copy.82), channel_id=1, source_target_pairs={{0,7},{1,0},{2,1},{3,2},{4,3},{5,4},{6,5},{7,6},{8,15},{9,8},{10,9... | collective-permute-start | bytes 589832 | tf_op jit(solution)/shard_map/while/body/eval_jaxpr/ppermute | solution.py:16
  345.2 11.0 %collective-permute-start.1 = (bf16[128,768]{0,1:T(8,128)(2,1)}, bf16[128,768]{0,1:T(8,128)(2,1)}, u32[]{:S(2)}, u32[]{:S(2)}) collective-permute-start(bf16[128,768]{0,1:T(8,128)(2,1)} %copy.83), channel_id=1, source_target_pairs={{0,7},{1,0},{2,1},{3,2},{4,3},{5,4},{6,5},{7,6},{8,15},{9,8},{10,9... | collective-permute-start | bytes 589832 | tf_op jit(solution)/shard_map/while/body/eval_jaxpr/ppermute | solution.py:16
  346.0 8.1 %collective-permute-start.2 = (bf16[128,768]{0,1:T(8,128)(2,1)}, bf16[128,768]{0,1:T(8,128)(2,1)S(1)}, u32[]{:S(2)}, u32[]{:S(2)}) collective-permute-start(bf16[128,768]{0,1:T(8,128)(2,1)} %fusion.105), channel_id=1, source_target_pairs={{0,7},{1,0},{2,1},{3,2},{4,3},{5,4},{6,5},{7,6},{8,15},{9,8},{10,9... | collective-permute-start | bytes 589832 | tf_op jit(solution)/shard_map/while/body/eval_jaxpr/ppermute | solution.py:16
  357.8 16.2 %collective-permute-start = (bf16[128,768]{0,1:T(8,128)(2,1)}, bf16[128,768]{0,1:T(8,128)(2,1)}, u32[]{:S(2)}, u32[]{:S(2)}) collective-permute-start(bf16[128,768]{0,1:T(8,128)(2,1)} %copy.82), channel_id=1, source_target_pairs={{0,7},{1,0},{2,1},{3,2},{4,3},{5,4},{6,5},{7,6},{8,15},{9,8},{10,9... | collective-permute-start | bytes 589832 | tf_op jit(solution)/shard_map/while/body/eval_jaxpr/ppermute | solution.py:16
  363.1 10.9 %collective-permute-start.1 = (bf16[128,768]{0,1:T(8,128)(2,1)}, bf16[128,768]{0,1:T(8,128)(2,1)}, u32[]{:S(2)}, u32[]{:S(2)}) collective-permute-start(bf16[128,768]{0,1:T(8,128)(2,1)} %copy.83), channel_id=1, source_target_pairs={{0,7},{1,0},{2,1},{3,2},{4,3},{5,4},{6,5},{7,6},{8,15},{9,8},{10,9... | collective-permute-start | bytes 589832 | tf_op jit(solution)/shard_map/while/body/eval_jaxpr/ppermute | solution.py:16
  363.9 8.0 %collective-permute-start.2 = (bf16[128,768]{0,1:T(8,128)(2,1)}, bf16[128,768]{0,1:T(8,128)(2,1)S(1)}, u32[]{:S(2)}, u32[]{:S(2)}) collective-permute-start(bf16[128,768]{0,1:T(8,128)(2,1)} %fusion.105), channel_id=1, source_target_pairs={{0,7},{1,0},{2,1},{3,2},{4,3},{5,4},{6,5},{7,6},{8,15},{9,8},{10,9... | collective-permute-start | bytes 589832 | tf_op jit(solution)/shard_map/while/body/eval_jaxpr/ppermute | solution.py:16
  375.6 16.3 %collective-permute-start = (bf16[128,768]{0,1:T(8,128)(2,1)}, bf16[128,768]{0,1:T(8,128)(2,1)}, u32[]{:S(2)}, u32[]{:S(2)}) collective-permute-start(bf16[128,768]{0,1:T(8,128)(2,1)} %copy.82), channel_id=1, source_target_pairs={{0,7},{1,0},{2,1},{3,2},{4,3},{5,4},{6,5},{7,6},{8,15},{9,8},{10,9... | collective-permute-start | bytes 589832 | tf_op jit(solution)/shard_map/while/body/eval_jaxpr/ppermute | solution.py:16
  381.0 10.9 %collective-permute-start.1 = (bf16[128,768]{0,1:T(8,128)(2,1)}, bf16[128,768]{0,1:T(8,128)(2,1)}, u32[]{:S(2)}, u32[]{:S(2)}) collective-permute-start(bf16[128,768]{0,1:T(8,128)(2,1)} %copy.83), channel_id=1, source_target_pairs={{0,7},{1,0},{2,1},{3,2},{4,3},{5,4},{6,5},{7,6},{8,15},{9,8},{10,9... | collective-permute-start | bytes 589832 | tf_op jit(solution)/shard_map/while/body/eval_jaxpr/ppermute | solution.py:16
  381.8 8.0 %collective-permute-start.2 = (bf16[128,768]{0,1:T(8,128)(2,1)}, bf16[128,768]{0,1:T(8,128)(2,1)S(1)}, u32[]{:S(2)}, u32[]{:S(2)}) collective-permute-start(bf16[128,768]{0,1:T(8,128)(2,1)} %fusion.105), channel_id=1, source_target_pairs={{0,7},{1,0},{2,1},{3,2},{4,3},{5,4},{6,5},{7,6},{8,15},{9,8},{10,9... | collective-permute-start | bytes 589832 | tf_op jit(solution)/shard_map/while/body/eval_jaxpr/ppermute | solution.py:16
  393.6 16.2 %collective-permute-start = (bf16[128,768]{0,1:T(8,128)(2,1)}, bf16[128,768]{0,1:T(8,128)(2,1)}, u32[]{:S(2)}, u32[]{:S(2)}) collective-permute-start(bf16[128,768]{0,1:T(8,128)(2,1)} %copy.82), channel_id=1, source_target_pairs={{0,7},{1,0},{2,1},{3,2},{4,3},{5,4},{6,5},{7,6},{8,15},{9,8},{10,9... | collective-permute-start | bytes 589832 | tf_op jit(solution)/shard_map/while/body/eval_jaxpr/ppermute | solution.py:16
  398.9 10.9 %collective-permute-start.1 = (bf16[128,768]{0,1:T(8,128)(2,1)}, bf16[128,768]{0,1:T(8,128)(2,1)}, u32[]{:S(2)}, u32[]{:S(2)}) collective-permute-start(bf16[128,768]{0,1:T(8,128)(2,1)} %copy.83), channel_id=1, source_target_pairs={{0,7},{1,0},{2,1},{3,2},{4,3},{5,4},{6,5},{7,6},{8,15},{9,8},{10,9... | collective-permute-start | bytes 589832 | tf_op jit(solution)/shard_map/while/body/eval_jaxpr/ppermute | solution.py:16
  399.7 8.0 %collective-permute-start.2 = (bf16[128,768]{0,1:T(8,128)(2,1)}, bf16[128,768]{0,1:T(8,128)(2,1)S(1)}, u32[]{:S(2)}, u32[]{:S(2)}) collective-permute-start(bf16[128,768]{0,1:T(8,128)(2,1)} %fusion.105), channel_id=1, source_target_pairs={{0,7},{1,0},{2,1},{3,2},{4,3},{5,4},{6,5},{7,6},{8,15},{9,8},{10,9... | collective-permute-start | bytes 589832 | tf_op jit(solution)/shard_map/while/body/eval_jaxpr/ppermute | solution.py:16
  410.0 11.4 %collective-permute-start.5 = (bf16[128,768]{0,1:T(8,128)(2,1)S(1)}, bf16[128,768]{0,1:T(8,128)(2,1)S(1)}, u32[]{:S(2)}, u32[]{:S(2)}) collective-permute-start(bf16[128,768]{0,1:T(8,128)(2,1)S(1)} %add_convert_fusion), channel_id=1, source_target_pairs={{0,7},{1,0},{2,1},{3,2},{4,3},{5,4},{6,5},{7,6},{8,15},{9,8},{10,9... | collective-permute-start | bytes 589832 | tf_op jit(solution)/shard_map/ppermute | solution.py:16
  426.6 120.4 %all-reduce.4.cloned.1.call-start = ((), (), s32[]{:S(2)}) async-start(), calls=%async_computation.15 | async-start | bytes 5308416 | tf_op jit(solution)/shard_map/psum | solution.py:260
  427.4 191.8 %all-gather.21.cloned.1.call-start = ((), (), s32[]{:S(2)}) async-start(), calls=%async_computation.14 | async-start | bytes 7962624 | tf_op jit(solution)/shard_map/all_gather | solution.py:257
  (50 other events, 1117.4 us)
Sparse Core Ops, SparseCore 0:
  9.9 49.8 all-gather.8
  63.3 25.2 all-gather.10
  90.2 24.3 all-gather.12
  116.4 26.7 all-gather.14
  144.8 56.9 all-gather.16
  203.5 56.9 all-gather.18
  270.2 28.6 reduce-scatter.6
  301.9 56.9 reduce-scatter.8
  361.9 56.9 reduce-scatter.10
  426.8 47.6 reduce-scatter.4
  477.0 69.9 all-reduce.3
  548.5 70.5 all-gather.20
